TPU v7x, 32 devices: a whole 2x2x4 slice. The times are simulated.
32 devices in a mesh: gy: 4 (over y, x), gz: 8 (over z, core).
Axes of the slice: x: 2, y: 2, z: 4, core: 2. Of those that a mesh axis runs over, the one named last changes fastest.
Arguments:
- volume: float32 [128, 512, 128], P('gy', 'gz'), may hold values from -60 to 60
- cotangent: float32 [128, 512, 128], P('gy', 'gz'), may hold values from -96 to 96
Outputs:
- volume_grad: float32 [128, 512, 128], P('gy', 'gz')
All inputs are finite; a program needn't handle non-finite values.
Results may differ from a plain program's by a relative error of at most 0.0045.
Values sent between devices are 32-bit elements; how exact they have to be, the bound alone decides.
A program may use at most 128 MiB of HBM per device.

v0:
```python
import math

import jax
import jax.numpy as jnp
import numpy as np
from jax import lax
from jax.sharding import PartitionSpec as P

sigma_sq = 4.0
x_orders = [2, 0, 0, 1, 1, 0]
y_orders = [0, 2, 0, 1, 0, 1]
z_orders = [0, 0, 2, 0, 1, 1]


def with_halo(block, sides, width):
    for axis, dim in sides:
        count = lax.axis_size(axis)
        forward = [(i, i + 1) for i in range(count - 1)]
        backward = [(target, source) for source, target in forward]
        low = lax.ppermute(
            lax.slice_in_dim(block, block.shape[dim] - width, None, axis=dim), axis, forward
        )
        high = lax.ppermute(lax.slice_in_dim(block, 0, width, axis=dim), axis, backward)
        block = jnp.concatenate([low, block, high], axis=dim)
    return block


def kernel_taps(order, flipped):
    base = [math.exp(-offset * offset / 8.0) for offset in range(-6, 7)]
    total = sum(base)
    gauss = [value / total for value in base]
    if order == 0:
        taps = gauss
    elif order == 1:
        taps = [-(offset / 4.0) * gauss[offset + 6] for offset in range(-6, 7)]
    else:
        taps = [(offset * offset / 16.0 - 0.25) * gauss[offset + 6] for offset in range(-6, 7)]
    if flipped:
        taps = taps[::-1]
    return taps


def band_matrix(order, width):
    taps = kernel_taps(order, False)
    matrix = np.zeros((width, width))
    for shift_by in range(-6, 7):
        matrix = matrix + taps[6 - shift_by] * np.eye(width, k=shift_by)
    return jnp.asarray(matrix, jnp.float32)


def slide(field, taps, axis, length):
    accum = taps[0] * lax.slice_in_dim(field, 0, length, axis=axis)
    for offset in range(1, 13):
        accum = accum + taps[offset] * lax.slice_in_dim(field, offset, offset + length, axis=axis)
    return accum


def z_passes(extended, planes):
    return jnp.stack([slide(extended, kernel_taps(order, False), 1, planes) for order in range(3)])


def forward_rows(along_z, rows, width):
    members = []
    for member in range(6):
        field = slide(along_z[z_orders[member]], kernel_taps(y_orders[member], False), 0, rows)
        field = sigma_sq * jnp.dot(
            field, band_matrix(x_orders[member], width), precision=lax.Precision.HIGHEST
        )
        members.append(field)
    return jnp.stack(members)


def back_x(grads, width):
    members = []
    for member in range(6):
        matrix = band_matrix(x_orders[member], width)
        members.append(sigma_sq * jnp.dot(grads[member], matrix.T, precision=lax.Precision.HIGHEST))
    return jnp.stack(members)


def transposed_group(stack, axis, pass_orders, group_orders, length):
    groups = [None, None, None]
    for member in range(6):
        partial_value = slide(stack[member], kernel_taps(pass_orders[member], True), axis, length)
        bucket = group_orders[member]
        groups[bucket] = partial_value if groups[bucket] is None else groups[bucket] + partial_value
    return jnp.stack(groups)


def transposed_final(stack, axis, length):
    result = slide(stack[0], kernel_taps(0, True), axis, length)
    for order in range(1, 3):
        result = result + slide(stack[order], kernel_taps(order, True), axis, length)
    return result


def vessel_field(comps):
    h_xx, h_yy, h_zz = (comps[0], comps[1], comps[2])
    h_xy, h_xz, h_yz = (comps[3], comps[4], comps[5])
    mean_diag = (h_xx + h_yy + h_zz) / 3.0
    dev_xx = h_xx - mean_diag
    dev_yy = h_yy - mean_diag
    dev_zz = h_zz - mean_diag
    spread_sq = (
        dev_xx * dev_xx
        + dev_yy * dev_yy
        + dev_zz * dev_zz
        + 2.0 * (h_xy * h_xy + h_xz * h_xz + h_yz * h_yz)
    )
    radius = jnp.sqrt(spread_sq / 6.0)
    determ = (
        dev_xx * (dev_yy * dev_zz - h_yz * h_yz)
        - h_xy * (h_xy * dev_zz - h_yz * h_xz)
        + h_xz * (h_xy * h_yz - dev_yy * h_xz)
    )
    cosine = jnp.clip(determ / (2.0 * radius * radius * radius), -0.999999, 0.999999)
    third = jnp.arccos(cosine) / 3.0
    upper = mean_diag + 2.0 * radius * jnp.cos(third)
    lower = mean_diag + 2.0 * radius * jnp.cos(third + 2.0 * math.pi / 3.0)
    middle = 3.0 * mean_diag - upper - lower
    ratio_a = middle * middle / (lower * lower + 1.0)
    ratio_b = upper * upper / jnp.sqrt(middle * middle * lower * lower + 1.0)
    strength = upper * upper + middle * middle + lower * lower
    return (
        (1.0 - jnp.exp(-2.0 * ratio_a)) * jnp.exp(-2.0 * ratio_b) * (1.0 - jnp.exp(-strength / 2.0))
    )


def vessel_grad(comps, cotangent):
    value, pullback = jax.vjp(vessel_field, comps)
    return pullback(cotangent)[0]


def rowwise_grad(comps, cotangent):
    mapped = lax.map(
        lambda bundle: vessel_grad(bundle[0], bundle[1]), (jnp.moveaxis(comps, 1, 0), cotangent)
    )
    return jnp.moveaxis(mapped, 0, 1)


def per_device(volume, cotangent):
    rows, planes, width = volume.shape
    extended = with_halo(volume, (("gz", 1),), 6)
    along_z = z_passes(extended, planes)
    along_z = with_halo(along_z, (("gy", 1),), 6)
    comps = forward_rows(along_z, rows, width)
    grads = rowwise_grad(comps, cotangent)
    back_comps = back_x(grads, width)
    padded = with_halo(back_comps, (("gy", 1),), 6)
    groups = transposed_group(padded, 0, y_orders, z_orders, rows)
    groups = with_halo(groups, (("gz", 2),), 6)
    result = transposed_final(groups, 1, planes)
    return result


def solution(mesh):
    placed = (P("gy", "gz", None), P("gy", "gz", None))
    return jax.shard_map(
        per_device, mesh=mesh, in_specs=placed, out_specs=P("gy", "gz", None), check_vma=False
    )
```

profile of v0, /device:TPU:1, one launch (start us, length us, event | category | flops | bytes accessed | tf_op | source)
XLA Modules:
  0.0 296.3 jit_solution(8268366435135978029)
XLA Ops:
  1.0 2.0 collective-permute-start.1
  3.0 4.5 %collective-permute-start = (f32[32,6,128]{2,1,0:T(8,128)S(1)}, f32[32,6,128]{2,1,0:T(8,128)S(1)}, u32[]{:S(2)}, u32[]{:S(2)}) collective-permute-start(f32[32,6,128]{2,1,0:T(8,128)S(1)} %get-tuple-element.105), channel_id=1, source_target_pairs={{0,1},{1,2},{2,3},{3,4},{4,5},{5,6},{6,7},{8,9},{9,10},{10,11},{11... | collective-permute-start | bytes 294920 | tf_op jit(solution)/shard_map/ppermute | solution.py:20
  9.4 5.7 %multiply_add_fusion.6 = f32[32,64,128]{2,1,0:T(8,128)S(1)} fusion(f32[32,64,128]{2,1,0:T(8,128)} %param.16, f32[32,70,128]{2,1,0:T(8,128)S(1)} %constant_dynamic-update-slice_fusion, f32[32,6,128]{2,1,0:T(8,128)S(1)} %collective-permute-done), kind=kLoop, calls=%fused_computation.723 | loop fusion | flops 8126464 | bytes 8486912 | tf_op jit(solution)/shard_map/add | solution.py:54
  15.2 1.8 multiply_add_fusion.5
  17.0 1.8 multiply_add_fusion.4
  19.9 3.9 %collective-permute-start.2 = (f32[3,6,64,128]{3,2,1,0:T(8,128)}, f32[3,6,64,128]{3,2,1,0:T(8,128)}, u32[]{:S(2)}, u32[]{:S(2)}) collective-permute-start(f32[3,6,64,128]{3,2,1,0:T(8,128)} %get-tuple-element.104), channel_id=1, source_target_pairs={{0,8},{8,16},{16,24},{1,9},{9,17},{17,25},{2,10},{10,18},{18,26},{... | collective-permute-start | bytes 1769480 | tf_op jit(solution)/shard_map/ppermute | solution.py:20
  23.8 1.5 collective-permute-start.3
  25.3 10.4 %collective-permute-done.2 = f32[3,6,64,128]{3,2,1,0:T(8,128)} collective-permute-done((f32[3,6,64,128]{3,2,1,0:T(8,128)}, f32[3,6,64,128]{3,2,1,0:T(8,128)}, u32[]{:S(2)}, u32[]{:S(2)}) %collective-permute-start.2) | collective-permute-done | bytes 589856 | tf_op jit(solution)/shard_map/ppermute | solution.py:20
  35.7 14.3 %collective-permute-done.3 = f32[3,6,64,128]{3,2,1,0:T(8,128)} collective-permute-done((f32[3,6,64,128]{3,2,1,0:T(8,128)}, f32[3,6,64,128]{3,2,1,0:T(8,128)}, u32[]{:S(2)}, u32[]{:S(2)}) %collective-permute-start.3) | collective-permute-done | bytes 589856 | tf_op jit(solution)/shard_map/ppermute | solution.py:23
  50.0 1.9 pad_maximum_fusion.1
  51.9 1.7 fusion.37
  53.7 1.7 fusion.35
  55.4 1.7 fusion.33
  57.2 1.8 fusion.31
  58.9 1.7 fusion.29
  60.7 1.8 fusion.27
  62.5 2.6 copy-done.4
  65.1 137.7 %while.12 = (s32[]{:T(128)}, f32[32,6,64,128]{3,2,0,1:T(8,128)}, f32[32,6,64,128]{3,2,0,1:T(8,128)}, f32[32,64,128]{2,1,0:T(8,128)}, s32[]{:T(128)}) while((s32[]{:T(128)}, f32[32,6,64,128]{3,2,0,1:T(8,128)}, f32[32,6,64,128]{3,2,0,1:T(8,128)}, f32[32,64,128]{2,1,0:T(8,128)}, s32[]{:T(128)}) %tuple.70), condition=%wide.region_1.2_spmd, body=%wide.region_0.1_spmd.sunk | while | flops 2777090 | bytes 2490953 | solution.py:135
  83.2 1.4 add_add_fusion.17
  100.5 1.4 add_add_fusion.17
  202.8 2.4 bitcast_dynamic-update-slice_fusion.6
  205.2 2.2 bitcast_dynamic-update-slice_fusion.5
  211.6 3.2 %collective-permute-start.4 = (f32[6,6,64,128]{3,2,1,0:T(8,128)S(1)}, f32[6,6,64,128]{3,2,1,0:T(8,128)S(1)}, u32[]{:S(2)}, u32[]{:S(2)}) collective-permute-start(f32[6,6,64,128]{3,2,1,0:T(8,128)S(1)} %get-tuple-element.94), channel_id=1, source_target_pairs={{0,8},{8,16},{16,24},{1,9},{9,17},{17,25},{2,10},{10,18},{18,26},{... | collective-permute-start | bytes 3538952 | tf_op jit(solution)/shard_map/ppermute | solution.py:20
  216.1 24.0 %collective-permute-done.4 = f32[6,6,64,128]{3,2,1,0:T(8,128)S(1)} collective-permute-done((f32[6,6,64,128]{3,2,1,0:T(8,128)S(1)}, f32[6,6,64,128]{3,2,1,0:T(8,128)S(1)}, u32[]{:S(2)}, u32[]{:S(2)}) %collective-permute-start.4) | collective-permute-done | bytes 1179680 | tf_op jit(solution)/shard_map/ppermute | solution.py:20
  240.1 26.2 %collective-permute-done.5 = f32[6,6,64,128]{3,2,1,0:T(8,128)S(1)} collective-permute-done((f32[6,6,64,128]{3,2,1,0:T(8,128)S(1)}, f32[6,6,64,128]{3,2,1,0:T(8,128)S(1)}, u32[]{:S(2)}, u32[]{:S(2)}) %collective-permute-start.5) | collective-permute-done | bytes 1179680 | tf_op jit(solution)/shard_map/ppermute | solution.py:23
  266.3 3.7 %fusion.111 = f32[1,32,64,128]{3,2,1,0:T(8,128)S(1)} fusion(f32[6,32,64,128]{3,2,1,0:T(8,128)S(1)} %get-tuple-element.117, f32[6,6,64,128]{3,2,1,0:T(8,128)S(1)} %collective-permute-done.5, f32[6,6,64,128]{3,2,1,0:T(8,128)S(1)} %collective-permute-done.4, f32[32,64,128]{2,1,0:T(8,128)S(1)} %get-tuple-element.118, f32[32,64,128]{2,1,0:T(8,128)S(1)} %get-tuple-element.116), kind=kLoop, calls=%fused_computation.320 | loop fusion | flops 19660800 | bytes 11796480 | tf_op jit(solution)/shard_map/add | solution.py:86
  270.0 7.5 %fusion.56 = (f32[1,32,64,128]{3,2,1,0:T(8,128)S(1)}, f32[1,32,64,128]{3,2,1,0:T(8,128)S(1)}) fusion(f32[6,32,64,128]{3,2,1,0:T(8,128)S(1)} %get-tuple-element.117, f32[6,6,64,128]{3,2,1,0:T(8,128)S(1)} %collective-permute-done.5, f32[6,6,64,128]{3,2,1,0:T(8,128)S(1)} %collective-permute-done.4, f32[32,64,128]{2,1,0:T(8,128)S(1)} %get-tuple-element.114, ...), kind=kLoop, calls=%fused_computation.265 | loop fusion | flops 39321600 | bytes 14942208 | tf_op jit(solution)/shard_map/add | solution.py:86
  277.6 2.9 collective-permute-start.6
  280.5 1.9 collective-permute-start.7
  282.5 2.8 collective-permute-done.6
  285.2 4.4 %collective-permute-done.7 = f32[3,32,6,128]{3,2,1,0:T(8,128)S(1)} collective-permute-done((f32[3,32,6,128]{3,2,1,0:T(8,128)S(1)}, f32[3,32,6,128]{3,2,1,0:T(8,128)S(1)}, u32[]{:S(2)}, u32[]{:S(2)}) %collective-permute-start.7) | collective-permute-done | bytes 294944 | tf_op jit(solution)/shard_map/ppermute | solution.py:23
  290.5 5.8 %fusion.259 = f32[32,64,128]{2,1,0:T(8,128)} fusion(f32[32,76,128]{2,1,0:T(8,128)S(1)} %get-tuple-element.97, f32[32,76,128]{2,1,0:T(8,128)S(1)} %get-tuple-element.98, f32[32,76,128]{2,1,0:T(8,128)S(1)} %get-tuple-element.96), kind=kLoop, calls=%fused_computation.469 | loop fusion | flops 20185088 | bytes 41943040 | tf_op jit(solution)/shard_map/add | solution.py:93
  (217 shorter events, 144.6 us)
Async XLA Ops:
  1.0 7.8 %collective-permute-start.1 = (f32[32,6,128]{2,1,0:T(8,128)S(1)}, f32[32,6,128]{2,1,0:T(8,128)S(1)}, u32[]{:S(2)}, u32[]{:S(2)}) collective-permute-start(f32[32,6,128]{2,1,0:T(8,128)S(1)} %get-tuple-element.106), channel_id=1, source_target_pairs={{1,0},{2,1},{3,2},{4,3},{5,4},{6,5},{7,6},{9,8},{10,9},{11,10},{12... | collective-permute-start | bytes 294920 | tf_op jit(solution)/shard_map/ppermute | solution.py:23
  3.0 6.5 %collective-permute-start = (f32[32,6,128]{2,1,0:T(8,128)S(1)}, f32[32,6,128]{2,1,0:T(8,128)S(1)}, u32[]{:S(2)}, u32[]{:S(2)}) collective-permute-start(f32[32,6,128]{2,1,0:T(8,128)S(1)} %get-tuple-element.105), channel_id=1, source_target_pairs={{0,1},{1,2},{2,3},{3,4},{4,5},{5,6},{6,7},{8,9},{9,10},{10,11},{11... | collective-permute-start | bytes 294920 | tf_op jit(solution)/shard_map/ppermute | solution.py:20
  8.9 6.3 %copy-start = (f32[32,64,128]{2,1,0:T(8,128)S(1)}, f32[32,64,128]{2,1,0:T(8,128)}, u32[]{:S(2)}) copy-start(f32[32,64,128]{2,1,0:T(8,128)} %param.16) | copy-start | bytes 3145732
  19.9 15.8 %collective-permute-start.2 = (f32[3,6,64,128]{3,2,1,0:T(8,128)}, f32[3,6,64,128]{3,2,1,0:T(8,128)}, u32[]{:S(2)}, u32[]{:S(2)}) collective-permute-start(f32[3,6,64,128]{3,2,1,0:T(8,128)} %get-tuple-element.104), channel_id=1, source_target_pairs={{0,8},{8,16},{16,24},{1,9},{9,17},{17,25},{2,10},{10,18},{18,26},{... | collective-permute-start | bytes 1769480 | tf_op jit(solution)/shard_map/ppermute | solution.py:20
  23.8 26.2 %collective-permute-start.3 = (f32[3,6,64,128]{3,2,1,0:T(8,128)}, f32[3,6,64,128]{3,2,1,0:T(8,128)}, u32[]{:S(2)}, u32[]{:S(2)}) collective-permute-start(f32[3,6,64,128]{3,2,1,0:T(8,128)} %get-tuple-element.103), channel_id=1, source_target_pairs={{8,0},{16,8},{24,16},{9,1},{17,9},{25,17},{10,2},{18,10},{26,18},{... | collective-permute-start | bytes 1769480 | tf_op jit(solution)/shard_map/ppermute | solution.py:23
  25.3 26.6 %copy-start.5 = (f32[128,128,1]{1,0,2:T(8,128)S(1)}, f32[128,128,1]{1,0,2:T(8,128)}, u32[]{:S(2)}) copy-start(f32[128,128,1]{1,0,2:T(8,128)} %constant.186) | copy-start | bytes 196612
  51.9 1.8 copy-start.2
  55.4 1.8 copy-start.3
  62.5 2.6 copy-start.4
  202.8 4.6 %copy-start.1 = (f32[32,6,64,128]{3,2,0,1:T(8,128)S(1)}, f32[32,6,64,128]{3,2,0,1:T(8,128)}, u32[]{:S(2)}) copy-start(f32[32,6,64,128]{3,2,0,1:T(8,128)} %get-tuple-element.59) | copy-start | bytes 18874372
  211.6 28.5 %collective-permute-start.4 = (f32[6,6,64,128]{3,2,1,0:T(8,128)S(1)}, f32[6,6,64,128]{3,2,1,0:T(8,128)S(1)}, u32[]{:S(2)}, u32[]{:S(2)}) collective-permute-start(f32[6,6,64,128]{3,2,1,0:T(8,128)S(1)} %get-tuple-element.94), channel_id=1, source_target_pairs={{0,8},{8,16},{16,24},{1,9},{9,17},{17,25},{2,10},{10,18},{18,26},{... | collective-permute-start | bytes 3538952 | tf_op jit(solution)/shard_map/ppermute | solution.py:20
  214.8 51.6 %collective-permute-start.5 = (f32[6,6,64,128]{3,2,1,0:T(8,128)S(1)}, f32[6,6,64,128]{3,2,1,0:T(8,128)S(1)}, u32[]{:S(2)}, u32[]{:S(2)}) collective-permute-start(f32[6,6,64,128]{3,2,1,0:T(8,128)S(1)} %get-tuple-element.95), channel_id=1, source_target_pairs={{8,0},{16,8},{24,16},{9,1},{17,9},{25,17},{10,2},{18,10},{26,18},{... | collective-permute-start | bytes 3538952 | tf_op jit(solution)/shard_map/ppermute | solution.py:23
  277.6 7.6 %collective-permute-start.6 = (f32[3,32,6,128]{3,2,1,0:T(8,128)S(1)}, f32[3,32,6,128]{3,2,1,0:T(8,128)S(1)}, u32[]{:S(2)}, u32[]{:S(2)}) collective-permute-start(f32[3,32,6,128]{3,2,1,0:T(8,128)S(1)} %get-tuple-element.99), channel_id=1, source_target_pairs={{0,1},{1,2},{2,3},{3,4},{4,5},{5,6},{6,7},{8,9},{9,10},{10,11},{11... | collective-permute-start | bytes 884744 | tf_op jit(solution)/shard_map/ppermute | solution.py:20
  280.5 9.1 %collective-permute-start.7 = (f32[3,32,6,128]{3,2,1,0:T(8,128)S(1)}, f32[3,32,6,128]{3,2,1,0:T(8,128)S(1)}, u32[]{:S(2)}, u32[]{:S(2)}) collective-permute-start(f32[3,32,6,128]{3,2,1,0:T(8,128)S(1)} %get-tuple-element.100), channel_id=1, source_target_pairs={{1,0},{2,1},{3,2},{4,3},{5,4},{6,5},{7,6},{9,8},{10,9},{11,10},{12... | collective-permute-start | bytes 884744 | tf_op jit(solution)/shard_map/ppermute | solution.py:23
where the time goes:
time: 302 us; the launch traced here: 296 us
  other arithmetic  137 us (45%)
  waiting for transfers between devices  82.7 us (27%)
  local copies, waits for them, and re-layouts  35.5 us (12%)
  starting transfers between devices  21.2 us (7%)
  matrix products  19 us (6%)
    ppermute x4, waiting for transfers between devices, with_halo(): lax.ppermute(lax.slice_in_dim(block, 0, width, axis=dim), axis, backward)  44.9 us
    add_any x32, other arithmetic, vessel_field(): h_yz * h_yz  43.3 us
    add_any x64, other arithmetic, vessel_field(): mean_diag = (h_xx + h_yy + h_zz) / 3.0  39.8 us
    ppermute x4, waiting for transfers between devices, with_halo(): lax.ppermute(lax.slice_in_dim(block, block.shape[dim] - width, None, axis...  37.8 us
    dynamic_slice x32, local copies, waits for them, and re-layouts, rowwise_grad(): lax.map(lambda bundle: vessel_grad(bundle[0], bundle[1]), (jnp.moveaxis(c...  30.1 us
    dynamic_update_slice x32, other arithmetic, rowwise_grad(): lax.map(lambda bundle: vessel_grad(bundle[0], bundle[1]), (jnp.moveaxis(c...  22.2 us
    ppermute x4, starting transfers between devices, with_halo(): lax.ppermute(lax.slice_in_dim(block, block.shape[dim] - width, None, axis...  14.6 us
    add x2, other arithmetic, transposed_group(): groups[bucket] + partial_value  11.2 us
  transfers between devices with their start and end apart: 8, of which 7 were waited for; matrix products, arithmetic and copies ran while one was open for 0% of the time, Pallas kernels for 0%

commit v1 on v0

v1 whole, which is shorter than its diff:
```python
import functools
import math

import jax
import jax.numpy as jnp
import numpy as np
from jax import lax
from jax.experimental import pallas as pl
from jax.experimental.pallas import tpu as pltpu
from jax.sharding import PartitionSpec as P

REACH = 6
PAD = 8
X_ORDERS = (2, 0, 0, 1, 1, 0)
SIDES = [(dy, dz) for dy in (-1, 0, 1) for dz in (-1, 0, 1) if (dy, dz) != (0, 0)]


def kernel_taps(order):
    base = [math.exp(-t * t / 8.0) for t in range(-REACH, REACH + 1)]
    total = sum(base)
    scale = (
        lambda t: 1.0,
        lambda t: -(t / 4.0),
        lambda t: t * t / 16.0 - 0.25,
    )[order]
    return [scale(t) * base[t + REACH] / total for t in range(-REACH, REACH + 1)]


TAPS = [kernel_taps(order)[REACH:] for order in range(3)]


def split_weights(width):
    stacks = []
    for flip in (False, True):
        for order in range(3):
            taps = kernel_taps(order)
            band = np.zeros((width, width))
            for shift in range(-REACH, REACH + 1):
                band = band + taps[REACH - shift] * np.eye(width, k=shift)
            rest = 4.0 * (band.T if flip else band)
            parts = []
            for _ in range(3):
                parts.append(rest.astype(jnp.bfloat16))
                rest = rest - parts[-1].astype(np.float64)
            b1, b2, b3 = parts
            top = np.concatenate([b1, b2, b3], axis=1)
            bottom = np.concatenate([b1, b2, b1], axis=1)
            stacks.append(np.concatenate([top, bottom], axis=0))
    return np.stack(stacks)


def spread_weights(planes):
    deep = planes + 2 * PAD
    band = np.zeros((deep, 3 * planes))
    for order in range(3):
        taps = kernel_taps(order)
        for t in range(-REACH, REACH + 1):
            band[:, order * planes : (order + 1) * planes] += taps[t + REACH] * np.eye(
                deep, planes, k=-PAD - t
            )
    high = band.astype(jnp.bfloat16)
    low = (band - high.astype(np.float64)).astype(jnp.bfloat16)
    return np.concatenate([high, low], axis=0)


def even(values, order):
    taps = TAPS[order]
    out = taps[0] * values[REACH]
    for t in range(1, REACH + 1):
        out = out + taps[t] * (values[REACH + t] + values[REACH - t])
    return out


def odd(values):
    taps = TAPS[1]
    out = taps[1] * (values[REACH + 1] - values[REACH - 1])
    for t in range(2, REACH + 1):
        out = out + taps[t] * (values[REACH + t] - values[REACH - t])
    return out


def passes(values, orders):
    evens = [order for order in orders if order != 1]
    out = {order: TAPS[order][0] * values[REACH] for order in evens}
    for t in range(1, REACH + 1):
        if evens:
            pair = values[REACH + t] + values[REACH - t]
            for order in evens:
                out[order] = out[order] + TAPS[order][t] * pair
    if 1 in orders:
        out[1] = odd(values)
    return out


ACOS = (
    1.5707963050,
    -0.2145988016,
    0.0889789874,
    -0.0501743046,
    0.0308918810,
    -0.0170881256,
    0.0066700901,
    -0.0012624911,
)


def horner(x, coefs):
    out = coefs[-1]
    for coef in coefs[-2::-1]:
        out = out * x + coef
    return out


def vessel_grads(hxx, hyy, hzz, hxy, hxz, hyz, cot):
    limit = np.float32(0.999999)
    mean = (hxx + hyy + hzz) * (1.0 / 3.0)
    dx, dy, dz = hxx - mean, hyy - mean, hzz - mean
    xy2, xz2, yz2 = hxy * hxy, hxz * hxz, hyz * hyz
    p2 = (dx * dx + dy * dy + dz * dz + 2.0 * (xy2 + xz2 + yz2)) * (1.0 / 6.0)
    p = jnp.sqrt(p2)
    inv = lax.rsqrt(p2)
    cxx = dy * dz - yz2
    cxy = hxz * hyz - hxy * dz
    cxz = hxy * hyz - dy * hxz
    cyz = hxy * hxz - dx * hyz
    cyy = dx * dz - xz2
    czz = dx * dy - xy2
    det = dx * cxx + hxy * cxy + hxz * cxz
    raw = det / (2.0 * p * p * p)
    size = jnp.abs(raw)
    positive = raw >= 0.0
    open_ = jnp.where(size < limit, 1.0, jnp.where(size == limit, 0.5, 0.0))
    size = jnp.minimum(size, limit)
    gap = 1.0 - size
    root = gap * lax.rsqrt(gap)
    psi = root * horner(size, [c / 3.0 for c in ACOS])
    sq = psi * psi
    cos = horner(sq, [1.0, -1.0 / 2, 1.0 / 24, -1.0 / 720, 1.0 / 40320])
    sin = psi * horner(sq, [1.0, -1.0 / 6, 1.0 / 120, -1.0 / 5040])
    wide = math.sqrt(3.0) * sin
    large, side = 2.0 * cos, cos + wide
    up = jnp.where(positive, large, side)
    low = jnp.where(positive, side, large)
    mid = low - up
    upper, lower, middle = mean + p * up, mean - p * low, mean + p * mid

    u2, m2, l2 = upper * upper, middle * middle, lower * lower
    ia = 1.0 / (l2 + 1.0)
    ra = m2 * ia
    w = lax.rsqrt(m2 * l2 + 1.0)
    rb = u2 * w
    e1 = jnp.exp(-2.0 * ra)
    e2 = jnp.exp(-2.0 * rb) * cot
    e3 = jnp.exp(-0.5 * (u2 + m2 + l2))
    f1, f3 = 1.0 - e1, 1.0 - e3
    ga = 4.0 * ia * (e1 * e2 * f3)
    f12 = f1 * e2
    gb = 2.0 * f12 * f3
    gs = f12 * e3
    bw = gb * rb * (w * w)
    fu = upper * (gs - 2.0 * gb * w)
    fm = middle * (ga + bw * l2 + gs)
    fl = lower * (gs - ga * ra + bw * m2)
    gu, gl = fu - fm, fl - fm
    third = (fu + fm + fl) * (1.0 / 3.0)
    bent = (math.sqrt(3.0) / 2.0) * cos - 0.5 * sin
    near_sin = jnp.where(positive, sin, bent)
    far_sin = jnp.where(positive, bent, sin)
    gr = (gu * near_sin + gl * far_sin) * (open_ * lax.rsqrt(gap * (1.0 + size)))
    gp = gu * up - gl * low - 2.0 * raw * gr
    along = gp * inv * (1.0 / 6.0)
    cof = gr * (1.0 / 3.0) * (inv * inv)
    third = third + cof * p2
    twice_along, twice_cof = 2.0 * along, 2.0 * cof
    return (
        along * dx + cof * cxx + third,
        along * dy + cof * cyy + third,
        along * dz + cof * czz + third,
        twice_along * hxy + twice_cof * cxy,
        twice_along * hxz + twice_cof * cxz,
        twice_along * hyz + twice_cof * cyz,
    )


def mix(block, weights, exact):
    width = block.shape[1]
    dot = functools.partial(jnp.dot, preferred_element_type=jnp.float32)
    high = block.astype(jnp.bfloat16)
    rest = block - high.astype(jnp.float32)
    low = rest.astype(jnp.bfloat16)
    out = dot(jnp.concatenate([high, low], axis=1), weights[:, : 2 * width])
    out, small = out[:, :width], out[:, width:]
    if exact:
        last = (rest - low.astype(jnp.float32)).astype(jnp.bfloat16)
        small = small + dot(jnp.concatenate([high, last], axis=1), weights[:, 2 * width :])
    return out + small


def kernel(
    ny, nz, vol, cot, weights, plane_weights, out, ext, smooth, hess, back, groups, edge,
    row_in, plane_in, corner_in, send1, recv1, send2, recv2,
):
    rows, planes, width = vol.shape
    tall = rows + 2 * REACH
    deep = planes + 2 * PAD
    gy, gz = lax.axis_index("gy"), lax.axis_index("gz")

    def has(dy, dz):
        ok = None
        for step, at, count in ((dy, gy, ny), (dz, gz, nz)):
            if step:
                one = (at > 0) if step < 0 else (at < count - 1)
                ok = one if ok is None else jnp.logical_and(ok, one)
        return ok

    ext[:REACH] = jnp.zeros((REACH, deep, width), jnp.float32)
    ext[rows + REACH :] = jnp.zeros((REACH, deep, width), jnp.float32)
    ext[REACH : rows + REACH, :PAD] = jnp.zeros((rows, PAD, width), jnp.float32)
    ext[REACH : rows + REACH, planes + PAD :] = jnp.zeros((rows, PAD, width), jnp.float32)
    row_in[...] = jnp.zeros_like(row_in)
    plane_in[...] = jnp.zeros_like(plane_in)
    corner_in[...] = jnp.zeros_like(corner_in)

    barrier = pltpu.get_barrier_semaphore()
    expected = jnp.int32(0)
    for dy, dz in SIDES:
        ok = has(dy, dz)
        expected = expected + jnp.where(ok, 1, 0)

        @pl.when(ok)
        def _(dy=dy, dz=dz):
            pl.semaphore_signal(
                barrier, inc=1, device_id=(gy + dy, gz + dz),
                device_id_type=pl.DeviceIdType.MESH,
            )

    pl.semaphore_wait(barrier, expected)

    def span(step, length, size):
        if step == 0:
            return pl.ds(0, length), pl.ds(size, length)
        if step > 0:
            return pl.ds(length - size, size), pl.ds(0, size)
        return pl.ds(0, size), pl.ds(length + size, size)

    def first(side, dy, dz):
        from_rows, to_rows = span(dy, rows, REACH)
        from_planes, to_planes = span(dz, planes, PAD)
        return pltpu.make_async_remote_copy(
            src_ref=vol.at[from_rows, from_planes, :],
            dst_ref=ext.at[to_rows, to_planes, :],
            send_sem=send1.at[side], recv_sem=recv1.at[side],
            device_id=(gy + dy, gz + dz), device_id_type=pl.DeviceIdType.MESH,
        )

    for side, (dy, dz) in enumerate(SIDES):
        @pl.when(has(dy, dz))
        def _(side=side, dy=dy, dz=dz):
            first(side, dy, dz).start()

    @pl.loop(0, rows)
    def _(r):
        ext[r + REACH, PAD : planes + PAD] = vol[r]

    for member in range(6):
        @pl.loop(0, 2 * REACH)
        def _(r):
            zero = jnp.zeros((planes, width), jnp.float32)
            back[member, r] = zero
            back[member, r + rows + 2 * REACH] = zero

    def opposite(side):
        return len(SIDES) - 1 - side

    for side, (dy, dz) in enumerate(SIDES):
        @pl.when(has(dy, dz))
        def _(side=side, dy=dy, dz=dz):
            first(side, dy, dz).wait_send()

        @pl.when(has(dy, dz))
        def _(side=side, dy=dy, dz=dz):
            back_side = opposite(side)
            first(back_side, -dy, -dz).wait_recv()

    @pl.loop(0, tall)
    def _(r):
        for c in range(0, planes, 16):
            start = c + PAD - REACH
            window = [ext[r, start + t : start + t + 16] for t in range(2 * REACH + 1)]
            done = passes(window, (0, 1, 2))
            for order in range(3):
                smooth[order, r, c : c + 16] = done[order]

    @pl.loop(0, rows // 4)
    def _(block):
        @pl.loop(0, planes // 8)
        def _(c):
            base = block * 4
            at = pl.ds(pl.multiple_of(c * 8, 8), 8)
            for order, todo in ((0, {0: 0, 2: 1, 1: 3}), (1, {0: 4, 1: 5}), (2, {0: 2})):
                held = [smooth[order, base + t, at] for t in range(2 * REACH + 4)]
                for r in range(4):
                    done = passes(held[r : r + 2 * REACH + 1], tuple(todo))
                    for y_order, member in todo.items():
                        hess[member, base + r, at] = done[y_order]

    @pl.loop(0, rows // 4)
    def _(block):
        at = pl.ds(block * 4, 4)
        for member in range(6):
            field = hess[member, at].reshape(4 * planes, width)
            field = mix(field, weights[X_ORDERS[member]], True)
            hess[member, at] = field.reshape(4, planes, width)

    @pl.loop(0, rows)
    def _(r):
        @pl.loop(0, planes // 16)
        def _(c):
            at = pl.ds(pl.multiple_of(c * 16, 16), 16)
            grads = vessel_grads(*[hess[m, r, at] for m in range(6)], cot[r, at])
            for member in range(6):
                hess[member, r, at] = grads[member]

    @pl.loop(0, rows // 4)
    def _(block):
        for member in range(6):
            field = hess[member, pl.ds(block * 4, 4)].reshape(4 * planes, width)
            field = mix(field, weights[3 + X_ORDERS[member]], False)
            back[member, pl.ds(block * 4 + 2 * REACH, 4)] = field.reshape(4, planes, width)

    def landing(dy, dz):
        if dy and dz:
            return corner_in.at[(dy + 1) // 2, (dz + 1) // 2]
        if dy:
            return row_in.at[(dy + 1) // 2]
        return plane_in.at[(dz + 1) // 2]

    def taken(step, length, size):
        if step == 0:
            return pl.ds(size, length)
        return pl.ds(length + size, size) if step > 0 else pl.ds(0, size)

    def second(side, dy, dz):
        return pltpu.make_async_remote_copy(
            src_ref=edge.at[taken(dy, rows, REACH), taken(dz, planes, PAD), :],
            dst_ref=landing(dy, dz),
            send_sem=send2.at[side], recv_sem=recv2.at[side],
            device_id=(gy + dy, gz + dz), device_id_type=pl.DeviceIdType.MESH,
        )

    def row_block(block):
        @pl.loop(0, planes // 8)
        def _(c):
            base = block * 4
            at = pl.ds(pl.multiple_of(c * 8, 8), 8)

            def held(member):
                return [back[member, base + t, at] for t in range(2 * REACH + 4)]

            for group, terms in (
                (0, ((0, 0), (1, 2), (3, 1))),
                (1, ((4, 0), (5, 1))),
                (2, ((2, 0),)),
            ):
                total = [None] * 4
                for member, order in terms:
                    values = held(member)
                    for r in range(4):
                        window = values[r : r + 2 * REACH + 1]
                        if order == 1:
                            total[r] = total[r] - odd(window)
                        elif total[r] is None:
                            total[r] = even(window, order)
                        else:
                            total[r] = total[r] + even(window, order)
                for r in range(4):
                    groups[base + r, pl.ds(pl.multiple_of(group * planes + c * 8, 8), 8)] = total[r]

        for n in range(4):
            r = block * 4 + n
            field = groups[r]
            high = field.astype(jnp.bfloat16)
            low = (field - high.astype(jnp.float32)).astype(jnp.bfloat16)
            both = jnp.concatenate([high, low], axis=1)
            done = jnp.dot(plane_weights[...], both, preferred_element_type=jnp.float32)
            edge[r] = done[:deep, :width] + done[:deep, width:] + done[deep:, :width]

    def send(wanted):
        for side, (dy, dz) in enumerate(SIDES):
            if wanted(dy):
                @pl.when(has(dy, dz))
                def _(side=side, dy=dy, dz=dz):
                    second(side, dy, dz).start()

    outer = -(-REACH // 4)
    blocks = tall // 4
    for block in [*range(outer), *range(blocks - outer, blocks)]:
        row_block(block)
    send(lambda dy: dy != 0)
    pl.loop(outer, blocks - outer)(row_block)
    send(lambda dy: dy == 0)

    @pl.loop(0, rows)
    def _(r):
        out[r] = edge[r + REACH, PAD : planes + PAD]

    for side, (dy, dz) in enumerate(SIDES):
        @pl.when(has(dy, dz))
        def _(side=side, dy=dy, dz=dz):
            second(side, dy, dz).wait_send()

        @pl.when(has(dy, dz))
        def _(side=side, dy=dy, dz=dz):
            second(opposite(side), -dy, -dz).wait_recv()

    for y, at_rows in ((1, slice(0, REACH)), (0, slice(rows - REACH, rows))):
        out[at_rows] = out[at_rows] + row_in[y]
    for z, at_planes in ((1, slice(0, PAD)), (0, slice(planes - PAD, planes))):
        out[:, at_planes] = out[:, at_planes] + plane_in[z]
        for y, at_rows in ((1, slice(0, REACH)), (0, slice(rows - REACH, rows))):
            out[at_rows, at_planes] = out[at_rows, at_planes] + corner_in[y, z]


def solution(mesh):
    ny, nz = mesh.shape["gy"], mesh.shape["gz"]

    def per_device(volume, cotangent):
        rows, planes, width = volume.shape
        tall, deep = rows + 2 * REACH, planes + 2 * PAD
        whole = pl.BlockSpec(memory_space=pltpu.VMEM)
        f32 = jnp.float32
        return pl.pallas_call(
            functools.partial(kernel, ny, nz),
            out_shape=jax.ShapeDtypeStruct(volume.shape, f32),
            in_specs=[whole] * 4,
            out_specs=whole,
            scratch_shapes=[
                pltpu.VMEM((tall, deep, width), f32),
                pltpu.VMEM((3, tall, planes, width), f32),
                pltpu.VMEM((6, rows, planes, width), f32),
                pltpu.VMEM((6, rows + 4 * REACH, planes, width), f32),
                pltpu.VMEM((tall, 3 * planes, width), f32),
                pltpu.VMEM((tall, deep, width), f32),
                pltpu.VMEM((2, REACH, planes, width), f32),
                pltpu.VMEM((2, rows, PAD, width), f32),
                pltpu.VMEM((2, 2, REACH, PAD, width), f32),
                pltpu.SemaphoreType.DMA((8,)),
                pltpu.SemaphoreType.DMA((8,)),
                pltpu.SemaphoreType.DMA((8,)),
                pltpu.SemaphoreType.DMA((8,)),
            ],
            compiler_params=pltpu.CompilerParams(
                collective_id=0, has_side_effects=True, vmem_limit_bytes=56 * 2**20
            ),
        )(volume, cotangent, jnp.asarray(split_weights(width)), jnp.asarray(spread_weights(planes)))

    placed = (P("gy", "gz", None), P("gy", "gz", None))
    return jax.shard_map(
        per_device, mesh=mesh, in_specs=placed, out_specs=P("gy", "gz", None), check_vma=False
    )
```

time: 302 us -> 64 us (0.21)
  the two profiles are of different devices: /device:TPU:1 before, /device:TPU:23 now
where the time goes in v1:
time: 64 us; the launch traced here: 63.8 us
  Pallas kernels  61.5 us (96%)
  local copies, waits for them, and re-layouts  2.31 us (4%)
    pallas_call x1, Pallas kernels, per_device(): pl.pallas_call(functools.partial(kernel, ny, nz), out_shape=jax.ShapeDtyp...  61.5 us
    unnamed x1, local copies, waits for them, and re-layouts  2.31 us

profile of v1, /device:TPU:23, one launch (start us, length us, event | category | flops | bytes accessed | tf_op | source)
XLA Modules:
  0.0 63.8 jit_solution(5003743483043407521)
XLA Ops:
  0.0 61.5 %shard_map.46 = f32[32,64,128]{2,1,0:T(8,128)} custom-call(f32[32,64,128]{2,1,0:T(8,128)} %vol.1, f32[32,64,128]{2,1,0:T(8,128)} %cot.1, bf16[6,256,384]{2,1,0:T(8,128)(2,1)} %constant.4.clone.weights, bf16[160,192]{1,0:T(8,128)(2,1)} %constant.5.clone.plane_weights), custom_call_target="tpu_custom_call" | custom-call | tf_op jit(solution)/shard_map/pallas_call | solution.py:432
  61.5 2.3 %copy.6 = f32[32,64,128]{2,1,0:T(8,128)} copy(f32[32,64,128]{2,1,0:T(8,128)} %shard_map.46) | data formatting | bytes 2097152

commit v2 on v1

--- a/solution.py
+++ b/solution.py
@@ -314,7 +314,7 @@
 
     @pl.loop(0, rows)
     def _(r):
-        @pl.loop(0, planes // 16)
+        @pl.loop(0, planes // 16, unroll=2)
         def _(c):
             at = pl.ds(pl.multiple_of(c * 16, 16), 16)
             grads = vessel_grads(*[hess[m, r, at] for m in range(6)], cot[r, at])

time: 64 us -> 60.1 us (0.939)
  Pallas kernels: 61.5 us -> 57.6 us
    pallas_call x1, Pallas kernels: 61.5 us -> 57.6 us  [per_device(): pl.pallas_call(functools.partial(kernel, ny, nz), out_shape=jax.ShapeDtyp...]
where the time goes in v2:
time: 60.1 us; the launch traced here: 59.9 us
  Pallas kernels  57.6 us (96%)
  local copies, waits for them, and re-layouts  2.31 us (4%)
    pallas_call x1, Pallas kernels, per_device(): pl.pallas_call(functools.partial(kernel, ny, nz), out_shape=jax.ShapeDtyp...  57.6 us
    unnamed x1, local copies, waits for them, and re-layouts  2.31 us

profile of v2, /device:TPU:23, one launch (start us, length us, event | category | flops | bytes accessed | tf_op | source)
XLA Modules:
  0.0 59.9 jit_solution(168145568140774705)
XLA Ops:
  0.0 57.6 %shard_map.46 = f32[32,64,128]{2,1,0:T(8,128)} custom-call(f32[32,64,128]{2,1,0:T(8,128)} %vol.1, f32[32,64,128]{2,1,0:T(8,128)} %cot.1, bf16[6,256,384]{2,1,0:T(8,128)(2,1)} %constant.4.clone.weights, bf16[160,192]{1,0:T(8,128)(2,1)} %constant.5.clone.plane_weights), custom_call_target="tpu_custom_call" | custom-call | tf_op jit(solution)/shard_map/pallas_call | solution.py:432
  57.6 2.3 %copy.6 = f32[32,64,128]{2,1,0:T(8,128)} copy(f32[32,64,128]{2,1,0:T(8,128)} %shard_map.46) | data formatting | bytes 2097152
